TPU v7x, 32 devices: a whole 2x2x4 slice. The times are simulated.
32 devices in a mesh: row: 4 (over y, x), col: 8 (over z, core).
Axes of the slice: x: 2, y: 2, z: 4, core: 2. Of those that a mesh axis runs over, the one named last changes fastest.
Arguments:
- trailing_grad: bfloat16 [4, 8, 768, 24576], P(None, 'col', None, 'row'), may hold values from -6 to 6
- panel: bfloat16 [24576, 512], P(('row', 'col')), may hold values from -0.0390625 to 0.0390625
- panel_grad: float32 [24576, 512], P(('row', 'col')), may hold values from -6 to 6
- diag_factor: float32 [512, 512], replicated, may hold values from -2 to 2, as said below
- diag_grad: float32 [512, 512], replicated, may hold values from -6 to 6
Outputs:
- panel_adj: float32 [24576, 512], P(('row', 'col'))
- diag_adj: float32 [512, 512], replicated
Inputs may be any that keep to these rules, and one draw needn't show every extreme that they name: `diag_factor`: lower triangular with zeros above the diagonal; diagonal entries between 1 and 2.
All inputs are finite; a program needn't handle non-finite values.
Results may differ from a plain program's by a relative error of at most 0.0003.
Values may be sent and summed in bfloat16 or wider, within the bound.
A program may use at most 128 MiB of HBM per device.

v0:
```python
import jax
import jax.numpy as jnp
from jax import lax
from jax.sharding import PartitionSpec as P


def halve_lower(matrix):
    rows = lax.broadcasted_iota(jnp.int32, matrix.shape, 0)
    cols = lax.broadcasted_iota(jnp.int32, matrix.shape, 1)
    keep = jnp.where(rows > cols, 1.0, jnp.where(rows == cols, 0.5, 0.0)).astype(jnp.float32)
    return matrix * keep


def keep_lower(matrix):
    rows = lax.broadcasted_iota(jnp.int32, matrix.shape, 0)
    cols = lax.broadcasted_iota(jnp.int32, matrix.shape, 1)
    return jnp.where(rows >= cols, matrix, 0.0)


def right_solve(left, lower):
    right = jax.scipy.linalg.solve_triangular(lower, left.T, lower=True, trans=1).T
    return 0.5 * (right + right.T)


def on_device(trailing_grad, panel, panel_grad, diag_factor, diag_grad):
    local_flip = trailing_grad.reshape(-1, trailing_grad.shape[3])
    lower = jnp.tril(diag_factor)
    col_panel = lax.all_gather(panel, "row", axis=0, tiled=True)
    row_panel = lax.all_gather(panel, "col", axis=0, tiled=True)
    block = local_flip
    direct = lax.psum_scatter(
        lax.dot_general(
            block, col_panel, (((0,), (0,)), ((), ())), preferred_element_type=jnp.float32
        ),
        "col",
        scatter_dimension=0,
        tiled=True,
    )
    block = local_flip
    transposed = lax.psum_scatter(
        jnp.dot(block, row_panel, preferred_element_type=jnp.float32),
        "row",
        scatter_dimension=0,
        tiled=True,
    )
    reduced = panel_grad - direct - transposed
    panel_adj = jax.scipy.linalg.solve_triangular(lower, reduced.T, lower=True, trans=1).T
    contrib = lax.dot_general(
        panel_adj,
        panel.astype(jnp.float32),
        (((0,), (0,)), ((), ())),
        precision=lax.Precision.HIGHEST,
    )
    diag_new = diag_grad - lax.psum(contrib, ("row", "col"))
    inner = halve_lower(jnp.dot(lower.T, keep_lower(diag_new), precision=lax.Precision.HIGHEST))
    left = jax.scipy.linalg.solve_triangular(lower, inner, lower=True, trans=1)
    return (panel_adj, right_solve(left, lower))


def solution(mesh):
    in_specs = (
        P(None, "col", None, "row"),
        P(("row", "col"), None),
        P(("row", "col"), None),
        P(),
        P(),
    )
    out_specs = (P(("row", "col"), None), P())
    return jax.shard_map(
        on_device, mesh=mesh, in_specs=in_specs, out_specs=out_specs, check_vma=False
    )
```

profile of v0, /device:TPU:0, one launch (start us, length us, event | category | flops | bytes accessed | tf_op | source)
XLA Modules:
  0.0 489.1 jit_solution(2284740775558172705)
XLA Ops:
  8.7 68.4 %all-gather.5.cloned.1.call-done = bf16[6144,512]{1,0:T(8,128)(2,1)} async-done(((bf16[768,512]{1,0:T(8,128)(2,1)}), bf16[6144,512]{1,0:T(8,128)(2,1)}) %all-gather.5.cloned.1.call-update) | async-done | bytes 6291472 | tf_op jit(solution)/shard_map/all_gather | solution.py:29
  77.1 26.8 %fusion.67 = f32[3072,512]{1,0:T(8,128)} fusion(bf16[3072,6144]{1,0:T(8,128)(2,1)} %bitcast.70, bf16[6144,512]{1,0:T(8,128)(2,1)} %all-gather.5.cloned.1.call-done), kind=kOutput, calls=%fused_computation.91 | convolution fusion | flops 19327352832 | bytes 50331648 | tf_op jit(solution)/shard_map/dot_general | solution.py:41
  103.9 17.5 %all-gather.3.cloned.1.call-done = bf16[3072,512]{1,0:T(8,128)(2,1)} async-done(((bf16[768,512]{1,0:T(8,128)(2,1)}), bf16[3072,512]{1,0:T(8,128)(2,1)}) %all-gather.3.cloned.1.call-update) | async-done | bytes 3145744 | tf_op jit(solution)/shard_map/all_gather | solution.py:28
  121.4 27.7 %fusion.66 = f32[6144,512]{1,0:T(8,128)} fusion(bf16[3072,6144]{1,0:T(8,128)(2,1)} %bitcast.71, bf16[3072,512]{1,0:T(8,128)(2,1)} %all-gather.3.cloned.1.call-done), kind=kOutput, calls=%fused_computation.90 | convolution fusion | flops 19327352832 | bytes 53477376 | tf_op jit(solution)/shard_map/dot_general | solution.py:32
  149.2 1.1 copy-done.6
  150.5 8.0 %while.5 = (s32[]{:T(128)}, f32[512,512]{1,0:T(8,128)S(1)}, s32[4,2]{0,1:T(2,128)S(1)}, f32[4,128,128]{2,1,0:T(8,128)S(1)}, s32[]{:T(128)}) while((s32[]{:T(128)}, f32[512,512]{1,0:T(8,128)S(1)}, s32[4,2]{0,1:T(2,128)S(1)}, f32[4,128,128]{2,1,0:T(8,128)S(1)}, s32[]{:T(128)}) %tuple.32), condition=%wide.while_cond.1, body=%wide.while_body.1.sunk | while | flops 2 | bytes 131181 | solution.py:47
  151.1 1.4 bitcast_dynamic-update-slice_fusion.2
  153.1 1.3 bitcast_dynamic-update-slice_fusion.2
  155.1 1.3 bitcast_dynamic-update-slice_fusion.2
  157.1 1.3 bitcast_dynamic-update-slice_fusion.2
  158.5 39.5 %custom-call.7 = f32[4,128,128]{1,2,0:T(8,128)S(1)} custom-call(f32[4,128,128]{2,1,0:T(8,128)S(1)} %get-tuple-element.18), custom_call_target="InvertDiagBlocksLowerTriangular" | custom-call | tf_op jit(solution)/shard_map/jit(_solve_triangular)/triangular_solve | solution.py:47
  198.0 127.9 %reduce-scatter.3.cloned.1.call-done = f32[768,512]{1,0:T(8,128)} async-done(((f32[6144,512]{1,0:T(8,128)}), f32[768,512]{1,0:T(8,128)}) %reduce-scatter.3.cloned.1.call-update) | async-done | bytes 1572880 | tf_op jit(solution)/shard_map/reduce_scatter | solution.py:31
  325.9 2.9 subtract_bitcast_fusion
  330.6 1.4 convolution_subtract_fusion.2
  332.5 2.1 convolution_subtract_fusion
  334.7 1.2 fusion.47
  335.9 3.4 fusion.10
  339.3 1.2 fusion.11
  340.5 1.6 copy.8
  342.2 126.4 %all-reduce.2.cloned.1.call-done = f32[512,512]{1,0:T(8,128)} async-done(((f32[512,512]{1,0:T(8,128)}), f32[512,512]{1,0:T(8,128)}) %all-reduce.2.cloned.1.call-update) | async-done | bytes 1048592 | tf_op jit(solution)/shard_map/psum | solution.py:54
  468.6 3.7 convolution_multiply_fusion
  477.1 1.0 convolution_subtract_fusion.3
  478.5 1.5 convolution_subtract_fusion.7
  481.4 1.2 add_multiply_fusion
  (55 shorter events, 12.9 us)
Async XLA Ops:
  7.2 69.9 %all-gather.5.cloned.1.call-start = ((), (), s32[]{:S(2)}) async-start(), calls=%async_computation.4 | async-start | bytes 7077888 | tf_op jit(solution)/shard_map/all_gather | solution.py:29
  7.9 113.5 %all-gather.3.cloned.1.call-start = ((), (), s32[]{:S(2)}) async-start(), calls=%async_computation.2 | async-start | bytes 3932160 | tf_op jit(solution)/shard_map/all_gather | solution.py:28
  8.6 189.3 %reduce-scatter.5.cloned.1.call-start = ((), (), s32[]{:S(2)}) async-start(), calls=%async_computation.5 | async-start | bytes 7864320 | tf_op jit(solution)/shard_map/reduce_scatter | solution.py:40
  103.8 222.1 %reduce-scatter.3.cloned.1.call-start = ((), (), s32[]{:S(2)}) async-start(), calls=%async_computation.3 | async-start | bytes 14155776 | tf_op jit(solution)/shard_map/reduce_scatter | solution.py:31
  149.1 1.2 copy-start.6
  149.1 319.4 %all-reduce.2.cloned.1.call-start = ((), (), s32[]{:S(2)}) async-start(), calls=%async_computation.6 | async-start | bytes 2097152 | tf_op jit(solution)/shard_map/psum | solution.py:54
  198.0 136.7 %copy-start.4 = (f32[4,128,128]{1,2,0:T(8,128)}, f32[4,128,128]{1,2,0:T(8,128)S(1)}, u32[]{:S(2)}) copy-start(f32[4,128,128]{1,2,0:T(8,128)S(1)} %custom-call.7) | copy-start | bytes 786436
  332.5 3.4 copy-start.2
  332.5 3.4 copy-start.3
  342.2 130.1 %copy-start.5 = (f32[4,128,128]{1,2,0:T(8,128)S(1)}, f32[4,128,128]{1,2,0:T(8,128)}, u32[]{:S(2)}) copy-start(f32[4,128,128]{1,2,0:T(8,128)} %copy-done.4) | copy-start | bytes 786436
  478.4 1.9 copy-start
  480.4 1.0 copy-start.1
Sparse Core Ops, SparseCore 0:
  9.6 67.4 all-gather.4
  78.9 42.4 all-gather.2
  124.4 70.1 reduce-scatter.4
  196.8 129.1 reduce-scatter.2
  339.4 129.0 all-reduce.1
where the time goes:
time: 489 us
  waiting for transfers between devices  342 us (70%)
  matrix products  76.4 us (16%)
  other arithmetic  45.1 us (9%)
  between operations  14.1 us (3%)
  local copies, waits for them, and re-layouts  11.6 us (2%)
    reduce_scatter x1, waiting for transfers between devices, on_device(): lax.psum_scatter(lax.dot_general(block, col_panel, (((0,), (0,)), ((), ()...  128 us
    psum x1, waiting for transfers between devices, on_device(): diag_new = diag_grad - lax.psum(contrib, ('row', 'col'))  126 us
    all_gather x1, waiting for transfers between devices, on_device(): row_panel = lax.all_gather(panel, 'col', axis=0, tiled=True)  68.4 us
    another operation x3, other arithmetic, on_device(): jax.scipy.linalg.solve_triangular(lower, reduced.T, lower=True, trans=1)  39.6 us
    dot_general x1, matrix products, on_device(): lax.dot_general(block, col_panel, (((0,), (0,)), ((), ())), preferred_ele...  27.7 us
    dot_general x1, matrix products, on_device(): jnp.dot(block, row_panel, preferred_element_type=jnp.float32)  26.8 us
    all_gather x1, waiting for transfers between devices, on_device(): col_panel = lax.all_gather(panel, 'row', axis=0, tiled=True)  17.5 us
  transfers between devices with their start and end apart: 5, of which 4 were waited for; matrix products, arithmetic and copies ran while one was open for 21% of the time, Pallas kernels for 0%

commit v1 on v0

v1 whole, which is shorter than its diff:
```python
import functools

import jax
import jax.numpy as jnp
from jax import lax
from jax.experimental import pallas as pl
from jax.experimental.pallas import tpu as pltpu
from jax.sharding import PartitionSpec as P

F32, BF16 = jnp.float32, jnp.bfloat16
VMEM_LIMIT = 66_000_000
NB = 4
BLK = 128
HI = lax.Precision.HIGHEST


def dot(a, b, ca=1, cb=0, precision=None):
    return lax.dot_general(
        a, b, (((ca,), (cb,)), ((), ())), precision=precision, preferred_element_type=F32
    )


def invert_blocks(l_ref, inv_ref):
    rows = lax.broadcasted_iota(jnp.int32, (BLK, BLK), 0)
    cols = lax.broadcasted_iota(jnp.int32, (BLK, BLK), 1)
    count = l_ref.shape[0] // BLK
    for j in range(count):
        block = l_ref[j * BLK : (j + 1) * BLK, j * BLK : (j + 1) * BLK]
        inv_ref[j] = jnp.where(rows == cols, 1.0 / jnp.where(rows == cols, block, 1.0), 0.0)

    def level(k, carry):
        same = (rows >> (k + 1)) == (cols >> (k + 1))
        mask = same & (((rows >> k) & 1) == 1) & (((cols >> k) & 1) == 0)
        for j in range(count):
            block = l_ref[j * BLK : (j + 1) * BLK, j * BLK : (j + 1) * BLK]
            x = inv_ref[j]
            y = dot(jnp.where(mask, block, 0.0), x, precision=HI)
            inv_ref[j] = x - dot(x, y, precision=HI)
        return carry

    lax.fori_loop(0, BLK.bit_length() - 1, level, 0)


def main_kernel(
    n_row, n_col, G, panel, panel_t, pg, low,
    dt_out, t_out, q_out, inv_out, pr, rl, tr,
    colp, rowp, gbuf, tacc, dsum, dpart, stage,
    gsem, cs, cr, zs, zr, ps, prr, ds, dr, rs, rr, ts, trs, lsem,
):
    nz = n_col // 2
    r, c = lax.axis_index("row"), lax.axis_index("col")
    z, k = c // 2, c % 2
    other = 2 * z + 1 - k
    g = panel.shape[0]
    last = nz - 1

    def dev(row, col):
        return dict(device_id=(row, col), device_id_type=pl.DeviceIdType.MESH)

    def tile_of(s):
        t = s - 2 * n_row
        i = t // n_row
        z_d = z_order(i // 2)
        c_d = 2 * z_d + jnp.where(i % 2 == 0, 1 - k, k)
        u = t - n_row * n_col
        rest = n_col - 2
        v = jnp.maximum(u, 0)
        a_b = (r + 1 + v // rest) % n_row
        jj = v % rest
        c_b = 2 * ((z + 1 + jj // 2) % nz) + jj % 2
        a = jnp.where(u >= 0, a_b, jnp.where(t >= 0, jnp.maximum(t, 0) % n_row, s % n_row))
        col = jnp.where(u >= 0, c_b, jnp.where(t >= 0, c_d, jnp.where(s < n_row, c, other)))
        return a, col

    def z_order(i):
        i = jnp.clip(i, 0, last)
        return jnp.where(z < nz // 2, last - i, i)

    total = 2 * n_row * n_col

    def tile_copy(s):
        a, col = tile_of(s)
        return pltpu.make_async_copy(
            G.at[pl.ds(pl.multiple_of(a * g, g), g), pl.ds(pl.multiple_of(col * g, g), g)],
            gbuf.at[s % NB],
            gsem.at[s % NB],
        )

    def next_tile(s):
        tile_copy(s).wait()

        @pl.when(s + NB - 1 < total)
        def _():
            tile_copy(s + NB - 1).start()

        a, col = tile_of(s)
        return a, col, gbuf[s % NB]

    for s in range(NB - 1):
        tile_copy(s).start()

    barrier = pltpu.get_barrier_semaphore()
    for d in range(1, n_row):
        pl.semaphore_signal(barrier, inc=1, **dev((r + d) % n_row, c))
    pl.semaphore_signal(barrier, inc=1, **dev(r, other))

    @pl.when(z > 0)
    def _():
        pl.semaphore_signal(barrier, inc=1, **dev(r, c - 2))

    @pl.when(z < last)
    def _():
        pl.semaphore_signal(barrier, inc=1, **dev(r, c + 2))

    near = jnp.where(z > 0, 1, 0) + jnp.where(z < last, 1, 0)
    pl.semaphore_wait(barrier, n_row + near)

    def col_send(d):
        return pltpu.make_async_remote_copy(
            panel_t, colp.at[r], cs.at[d], cr.at[d], **dev((r + d) % n_row, c)
        )

    def block_send(h, way, src):
        zb = z - (h - 1) if way == 0 else z + (h - 1)
        slot = 2 * zb + k
        return pltpu.make_async_remote_copy(
            rowp.at[slot] if src is None else src,
            rowp.at[slot],
            zs.at[way, h],
            zr.at[way, h],
            **dev(r, c + 2 if way == 0 else c - 2),
        )

    def pair_send(zb, src):
        slot = 2 * zb + k
        return pltpu.make_async_remote_copy(
            rowp.at[slot] if src is None else src, rowp.at[slot], ps.at[zb], prr.at[zb], **dev(r, other)
        )

    pair_send(z, panel).start()

    @pl.when(z < last)
    def _():
        block_send(1, 0, panel).start()

    @pl.when(z > 0)
    def _():
        block_send(1, 1, panel).start()

    for d in range(1, n_row):
        col_send(d).start()

    def relay(h):
        for way in range(2):
            zb = z - h if way == 0 else z + h
            have = (zb >= 0) if way == 0 else (zb <= last)
            onward = (z < last) if way == 0 else (z > 0)

            @pl.when(have)
            def _():
                pltpu.make_async_remote_copy(
                    panel, rowp.at[2 * zb + k], zs.at[way, h], zr.at[way, h], **dev(r, other)
                ).wait_recv()
                pair_send(zb, None).start()

                @pl.when(onward)
                def _():
                    block_send(h + 1, way, None).start()

    rowp[c] = panel[...]
    colp[r] = panel_t[...]

    def zero(a, carry):
        tacc[a] = jnp.zeros((g, panel.shape[1]), F32)
        return carry

    lax.fori_loop(0, n_row, zero, 0)

    def t_step(s, carry):
        a, col, tile = next_tile(s)
        tacc[a] += dot(tile, rowp[col])
        return carry

    lax.fori_loop(0, n_row, t_step, 0)

    def pair_wait(zb):
        pltpu.make_async_remote_copy(
            panel, rowp.at[2 * zb + 1 - k], ps.at[zb], prr.at[zb], **dev(r, other)
        ).wait_recv()

    pair_wait(z)
    lax.fori_loop(n_row, 2 * n_row, t_step, 0)
    invert_blocks(low, inv_out)
    relay(1)
    for d in range(1, n_row):
        pltpu.make_async_remote_copy(
            panel_t, colp.at[(r + n_row - d) % n_row], cs.at[d], cr.at[d], **dev((r + d) % n_row, c)
        ).wait_recv()

    def part_send(zb, slot):
        return pltpu.make_async_remote_copy(
            dpart.at[slot], pr.at[zb], ds.at[slot], dr.at[zb], **dev(r, other)
        )

    def sum_send(way, zb):
        return pltpu.make_async_remote_copy(
            dsum.at[zb], rl.at[way, zb], rs.at[way, zb], rr.at[way, zb],
            **dev(r, c + 2 if way == 0 else c - 2),
        )

    def add_in(dst, src):
        cp = pltpu.make_async_copy(src, stage, lsem)
        cp.start()
        cp.wait()
        dst[...] += stage[...]

    def presum(i):
        zb = z_order(i)
        part_send(zb, i % 2).wait_recv()
        add_in(dsum.at[zb], pr.at[zb])

        @pl.when((z == 0) & (zb > 0))
        def _():
            sum_send(0, zb).start()

        @pl.when((z == last) & (zb < last))
        def _():
            sum_send(1, zb).start()

    def d_into(base, ref):
        def step(j, carry):
            a, col, tile = next_tile(base + j)
            part = dot(colp[a], tile)

            @pl.when(j == 0)
            def _():
                ref[...] = part

            @pl.when(j > 0)
            def _():
                ref[...] += part

            return carry

        lax.fori_loop(0, n_row, step, 0)

    base = 2 * n_row
    for i in range(nz):
        zb = z_order(i)
        slot = i % 2
        if i >= 2:
            part_send(z_order(i - 2), slot).wait_send()
        d_into(base + 2 * i * n_row, dpart.at[slot])
        part_send(zb, slot).start()
        d_into(base + (2 * i + 1) * n_row, dsum.at[zb])
        presum(i)
        if i + 2 < nz:
            relay(i + 2)
    for h in range(nz + 1, nz):
        relay(h)

    def wait_others(d, carry):
        pair_wait((z + d) % nz)
        return carry

    lax.fori_loop(1, nz, wait_others, 0)

    def t_send(d):
        a = (r + d) % n_row
        return pltpu.make_async_remote_copy(
            tacc.at[a], tr.at[r], ts.at[d], trs.at[d], **dev(a, c)
        )

    base = 2 * n_row + n_row * n_col
    rest = n_col - 2
    for i in range(n_row):
        lax.fori_loop(base + i * rest, base + (i + 1) * rest, t_step, 0)
        if i < n_row - 1:
            t_send(i + 1).start()

    q_out[...] = jnp.zeros(q_out.shape, F32)

    def q_step(a, carry):
        t = tacc[a]
        hi = t.astype(BF16)
        lo = (t - hi.astype(F32)).astype(BF16)
        q_out[...] += dot(colp[a], hi) + dot(colp[a], lo)
        return carry

    lax.fori_loop(0, n_row, q_step, 0)

    def hop(way, zb):
        sum_wait = pltpu.make_async_remote_copy(
            stage, rl.at[way, zb], rs.at[way, zb], rr.at[way, zb], **dev(r, other)
        )
        sum_wait.wait_recv()
        add_in(dsum.at[zb], rl.at[way, zb])

    for q in range(nz):
        up = last - q

        @pl.when((z > 0) & (up > z))
        def _():
            hop(0, up)
            sum_send(0, up).start()

        @pl.when((z < last) & (q < z))
        def _():
            hop(1, q)
            sum_send(1, q).start()

    def fetch(src, dst):
        cp = pltpu.make_async_copy(src, dst, lsem)
        cp.start()
        cp.wait()

    t_out[...] = pg[...] - tacc[r]
    tbuf = tacc.at[(r + 1) % n_row]
    for d in range(1, n_row):
        t_send(d).wait_send()
    for d in range(1, n_row):
        src = (r + n_row - d) % n_row
        pltpu.make_async_remote_copy(
            tacc.at[src], tr.at[src], ts.at[d], trs.at[d], **dev((r + d) % n_row, c)
        ).wait_recv()
        fetch(tr.at[src], tbuf)
        t_out[...] -= tbuf[...]

    @pl.when(z > 0)
    def _():
        hop(0, z)

    @pl.when(z < last)
    def _():
        hop(1, z)

    dt_out[...] = dsum[z]

    for d in range(1, n_row):
        col_send(d).wait_send()
    for way in range(2):
        for h in range(1, nz):
            zb = z - (h - 1) if way == 0 else z + (h - 1)
            sent = ((zb >= 0) & (z < last)) if way == 0 else ((zb <= last) & (z > 0))

            @pl.when(sent)
            def _():
                block_send(h, way, panel).wait_send()

    for zb in range(nz):
        pair_send(zb, panel).wait_send()
        sent_up = z < zb
        sent_down = z > zb

        @pl.when(sent_up)
        def _():
            sum_send(0, zb).wait_send()

        @pl.when(sent_down)
        def _():
            sum_send(1, zb).wait_send()

    for i in range(max(nz - 2, 0), nz):
        part_send(z_order(i), i % 2).wait_send()


def main_call(G, panel, pg, low, n_row, n_col):
    g, b = panel.shape
    nz = n_col // 2
    vm = pl.BlockSpec(memory_space=pltpu.VMEM)
    hbm = pl.BlockSpec(memory_space=pl.ANY)
    dma = pltpu.SemaphoreType.DMA
    sds = jax.ShapeDtypeStruct
    sizes = [(NB,), (n_row,), (n_row,), (2, nz + 1), (2, nz + 1), (nz,), (nz,), (2,), (nz,),
             (2, nz), (2, nz), (n_row,), (n_row,)]
    flops = 4 * G.shape[0] * G.shape[1] * b
    outs = pl.pallas_call(
        functools.partial(main_kernel, n_row, n_col),
        out_shape=[
            sds((b, g), F32), sds((g, b), F32), sds((b, b), F32), sds((b // BLK, BLK, BLK), F32),
            sds((nz, b, g), F32), sds((2, nz, b, g), F32), sds((n_row, g, b), F32),
        ],
        in_specs=[hbm, vm, vm, vm, vm],
        out_specs=[vm, vm, vm, vm, hbm, hbm, hbm],
        scratch_shapes=[
            pltpu.VMEM((n_row, b, g), BF16),
            pltpu.VMEM((n_col, g, b), BF16),
            pltpu.VMEM((NB, g, g), BF16),
            pltpu.VMEM((n_row, g, b), F32),
            pltpu.VMEM((nz, b, g), F32),
            pltpu.VMEM((2, b, g), F32),
            pltpu.VMEM((b, g), F32),
        ]
        + [dma(s) for s in sizes]
        + [dma],
        compiler_params=pltpu.CompilerParams(
            collective_id=0, has_side_effects=True, vmem_limit_bytes=VMEM_LIMIT
        ),
        cost_estimate=pl.CostEstimate(flops=flops, bytes_accessed=4 * G.size, transcendentals=0),
    )(G, panel, panel.T, pg, low)
    return outs[:4]


def sum_kernel(n_row, n_col, x, out, a_in, a_sum, b_in, s1, r1, s2, r2, s3, r3, s4, r4):
    r, c = lax.axis_index("row"), lax.axis_index("col")

    def dev(row, col):
        return dict(device_id=(row, col), device_id_type=pl.DeviceIdType.MESH)

    def row_at(d):
        return lax.rem(r + d, n_row)

    def col_at(d):
        return lax.rem(c + d, n_col)

    barrier = pltpu.get_barrier_semaphore()
    for d in range(1, n_row):
        pl.semaphore_signal(barrier, inc=1, **dev(row_at(d), c))
    for d in range(1, n_col):
        pl.semaphore_signal(barrier, inc=1, **dev(r, col_at(d)))
    pl.semaphore_wait(barrier, n_row + n_col - 2)

    remote = pltpu.make_async_remote_copy
    one = [
        remote(x.at[row_at(d)], a_in.at[d], s1.at[d], r1.at[d], **dev(row_at(d), c))
        for d in range(1, n_row)
    ]
    for cp in one:
        cp.start()
    a_sum[...] = x[r]
    for cp, d in zip(one, range(1, n_row)):
        cp.wait_recv()
        a_sum[...] += a_in[d]
    two = [
        remote(a_sum.at[col_at(d)], b_in.at[d], s2.at[d], r2.at[d], **dev(r, col_at(d)))
        for d in range(1, n_col)
    ]
    for cp in two:
        cp.start()
    acc = a_sum[c]
    for cp, d in zip(two, range(1, n_col)):
        cp.wait_recv()
        acc += b_in[d]
    out[r, c] = acc
    three = [
        remote(out.at[r, c], out.at[r, c], s3.at[d], r3.at[d], **dev(r, col_at(d)))
        for d in range(1, n_col)
    ]
    for cp in three:
        cp.start()
    for d in range(1, n_col):
        remote(
            out.at[r, c], out.at[r, col_at(n_col - d)], s3.at[d], r3.at[d], **dev(r, col_at(d))
        ).wait_recv()
    four = [
        remote(out.at[r], out.at[r], s4.at[d], r4.at[d], **dev(row_at(d), c))
        for d in range(1, n_row)
    ]
    for cp in four:
        cp.start()
    for d in range(1, n_row):
        remote(
            out.at[r], out.at[row_at(n_row - d)], s4.at[d], r4.at[d], **dev(row_at(d), c)
        ).wait_recv()
    for cp in one + two + three + four:
        cp.wait_send()


def sum_call(x, n_row, n_col):
    shape = x.shape
    w = x.size // (n_row * n_col * 8)
    x = x.reshape(n_row, n_col, 8, w)
    vm = pl.BlockSpec(memory_space=pltpu.VMEM)
    dma = pltpu.SemaphoreType.DMA
    row, col = dma((n_row,)), dma((n_col,))
    out = pl.pallas_call(
        functools.partial(sum_kernel, n_row, n_col),
        out_shape=jax.ShapeDtypeStruct(x.shape, F32),
        in_specs=[vm],
        out_specs=vm,
        scratch_shapes=[
            pltpu.VMEM((n_row, n_col, 8, w), F32),
            pltpu.VMEM((n_col, 8, w), F32),
            pltpu.VMEM((n_col, 8, w), F32),
            row, row, col, col, col, col, row, row,
        ],
        compiler_params=pltpu.CompilerParams(collective_id=1, has_side_effects=True),
    )(x)
    return out.reshape(shape)


def right_blocks(rhs, low, inv):
    n = low.shape[0] // BLK
    part = lambda j: slice(j * BLK, (j + 1) * BLK)
    xs = [None] * n
    for j in reversed(range(n)):
        acc = rhs[:, part(j)]
        if j < n - 1:
            done = jnp.concatenate(xs[j + 1 :], axis=1)
            acc = acc - dot(done, low[(j + 1) * BLK :, part(j)], precision=HI)
        xs[j] = dot(acc, inv[j], precision=HI)
    return jnp.concatenate(xs, axis=1)


def left_blocks(rhs, low, inv):
    n = low.shape[0] // BLK
    part = lambda j: slice(j * BLK, (j + 1) * BLK)
    xs = [None] * n
    for j in reversed(range(n)):
        acc = rhs[part(j), :]
        if j < n - 1:
            done = jnp.concatenate(xs[j + 1 :], axis=0)
            acc = acc - dot(low[(j + 1) * BLK :, part(j)], done, 0, 0, precision=HI)
        xs[j] = dot(inv[j], acc, 0, 0, precision=HI)
    return jnp.concatenate(xs, axis=0)


def panel_kernel(t_ref, dt_ref, low, inv, out):
    out[...] = right_blocks(t_ref[...] - dt_ref[...].T, low[...], inv[...])


def diag_kernel(s_ref, dg, low, inv, out):
    lower, inverse = low[...], inv[...]
    rows = lax.broadcasted_iota(jnp.int32, lower.shape, 0)
    cols = lax.broadcasted_iota(jnp.int32, lower.shape, 1)
    diag_new = dg[...] - left_blocks(s_ref[...], lower, inverse)
    inner = dot(lower, jnp.where(rows >= cols, diag_new, 0.0), 0, 0, precision=HI)
    inner = inner * jnp.where(rows > cols, 1.0, jnp.where(rows == cols, 0.5, 0.0))
    right = right_blocks(left_blocks(inner, lower, inverse), lower, inverse)
    out[...] = 0.5 * (right + right.T)


def local_call(body, shape, *args):
    vm = pl.BlockSpec(memory_space=pltpu.VMEM)
    return pl.pallas_call(
        body,
        out_shape=jax.ShapeDtypeStruct(shape, F32),
        in_specs=[vm] * len(args),
        out_specs=vm,
        compiler_params=pltpu.CompilerParams(vmem_limit_bytes=48_000_000),
    )(*args)


def plain_products(block, panel, panel_grad, lower):
    col_panel = lax.all_gather(panel, "row", axis=0, tiled=True)
    row_panel = lax.all_gather(panel, "col", axis=0, tiled=True)
    direct = lax.psum_scatter(dot(block, col_panel, 0, 0), "col", scatter_dimension=0, tiled=True)
    part = dot(block, row_panel)
    transposed = lax.psum_scatter(part, "row", scatter_dimension=0, tiled=True)
    high = part.astype(BF16)
    q = dot(col_panel, high, 0, 0) + dot(col_panel, (part - high.astype(F32)).astype(BF16), 0, 0)
    inv = local_call(invert_blocks, (lower.shape[0] // BLK, BLK, BLK), lower)
    return direct.T, panel_grad - transposed, q, inv


def on_device(n_row, n_col, trailing_grad, panel, panel_grad, diag_factor, diag_grad):
    local_flip = trailing_grad.reshape(-1, trailing_grad.shape[3])
    lower = jnp.tril(diag_factor)
    own = dot(panel_grad, panel.astype(F32), 0, 0, precision=HI)
    if panel.shape[0] % 128 == 0 and n_col % 2 == 0 and n_col > 2:
        dt, t, q, inv = main_call(local_flip, panel, panel_grad, lower, n_row, n_col)
    else:
        dt, t, q, inv = plain_products(local_flip, panel, panel_grad, lower)
    total = sum_call(own - q - q.T, n_row, n_col)
    panel_adj = local_call(panel_kernel, panel_grad.shape, t, dt, lower, inv)
    diag_adj = local_call(diag_kernel, lower.shape, total, diag_grad, lower, inv)
    return (panel_adj, diag_adj)


def solution(mesh):
    in_specs = (
        P(None, "col", None, "row"),
        P(("row", "col"), None),
        P(("row", "col"), None),
        P(),
        P(),
    )
    out_specs = (P(("row", "col"), None), P())
    body = functools.partial(on_device, mesh.shape["row"], mesh.shape["col"])
    return jax.shard_map(body, mesh=mesh, in_specs=in_specs, out_specs=out_specs, check_vma=False)
```

time: 489 us -> 301 us (0.62)
  waiting for transfers between devices: 342 us -> 0 us
  Pallas kernels: 0 us -> 284 us
  matrix products: 76.4 us -> 3.11 us
  other arithmetic: 45.1 us -> 1.1 us
  between operations: 14.1 us -> 0.73 us
    pallas_call x0 -> x4, Pallas kernels: none -> 284 us  [the longest x1 218 us: main_call(): pl.pallas_call(functools.partial(main_kernel, n_row, n_col), out_shape=[s...]
    reduce_scatter x2 -> x0, waiting for transfers between devices: 128 us -> none  [the longest x1 128 us: on_device(): lax.psum_scatter(lax.dot_general(block, col_panel, (((0,), (0,)), ((), ()...]
    psum x1 -> x0, waiting for transfers between devices: 126 us -> none  [on_device(): diag_new = diag_grad - lax.psum(contrib, ('row', 'col'))]
    all_gather x2 -> x0, waiting for transfers between devices: 85.9 us -> none  [the longest x1 68.4 us: on_device(): row_panel = lax.all_gather(panel, 'col', axis=0, tiled=True)]
    dot_general x4 -> x1, matrix products: 61.6 us -> 3.11 us  [dot(): lax.dot_general(a, b, (((ca,), (cb,)), ((), ())), precision=precision, pr...]
    another operation x3 -> x0, other arithmetic: 39.6 us -> none  [on_device(): jax.scipy.linalg.solve_triangular(lower, reduced.T, lower=True, trans=1)]
    another operation x21 -> x0, matrix products: 14.8 us -> none  [the longest x7 6.99 us: on_device(): jax.scipy.linalg.solve_triangular(lower, reduced.T, lower=True, trans=1)]
    another operation x13 -> x0, local copies, waits for them, and re-layouts: 7.88 us -> none
  transfers between devices with their start and end apart: 5 -> 0, of which waited for: 4 -> 0; matrix products, arithmetic and copies ran while one was open for 21% -> 0% of each run, Pallas kernels for 0% -> 0%
where the time goes in v1:
time: 301 us; the launch traced here: 300 us
  Pallas kernels  284 us (94%)
  local copies, waits for them, and re-layouts  11.2 us (4%)
  matrix products  3.11 us (1%)
    pallas_call x1, Pallas kernels, main_call(): pl.pallas_call(functools.partial(main_kernel, n_row, n_col), out_shape=[s...  218 us
    pallas_call x1, Pallas kernels, sum_call(): pl.pallas_call(functools.partial(sum_kernel, n_row, n_col), out_shape=jax...  46.6 us
    pallas_call x2, Pallas kernels, local_call(): pl.pallas_call(body, out_shape=jax.ShapeDtypeStruct(shape, F32), in_specs...  19.5 us
    unnamed x19, local copies, waits for them, and re-layouts  7.64 us

profile of v1, /device:TPU:0, one launch (start us, length us, event | category | flops | bytes accessed | tf_op | source)
XLA Modules:
  0.0 300.3 jit_solution(8018135143097504865)
XLA Ops:
  0.6 0.0 copy-start.8
  0.6 2.4 copy.7
  3.0 0.0 copy-done.8
  3.0 1.1 fusion.1.low
  4.1 218.1 %shard_map.68 = (f32[512,768]{1,0:T(8,128)}, f32[768,512]{1,0:T(8,128)}, f32[512,512]{1,0:T(8,128)}, f32[4,128,128]{2,1,0:T(8,128)}, f32[4,512,768]{2,1,0:T(8,12...) custom-call(bf16[3072,6144]{1,0:T(8,128)(2,1)} %bitcast.9, bf16[768,512]{1,0:T(8,128)(2,1)} %panel.1, ...), custom_call_target="tpu_custom_call" | custom-call | flops 38654705664 | bytes 75497472 | tf_op jit(solution)/shard_map/pallas_call | solution.py:377
  222.2 0.0 copy-start
  222.2 1.2 copy-done
  223.5 1.4 copy-done.2
  224.9 1.4 copy-done.3
  226.3 0.9 copy-done.5
  227.2 7.0 %shard_map.69 = f32[768,512]{1,0:T(8,128)} custom-call(f32[768,512]{1,0:T(8,128)S(1)} %copy-done.3, f32[512,768]{1,0:T(8,128)S(1)} %copy-done.2, f32[512,512]{1,0:T(8,128)S(1)} %copy-done, f32[4,128,128]{2,1,0:T(8,128)S(1)} %copy-done.5), custom_call_target="tpu_custom_call" | custom-call | tf_op jit(solution)/shard_map/pallas_call | solution.py:535
  234.2 0.0 copy-done.7
  234.2 0.3 copy.9
  234.6 3.1 %fusion = f32[512,512]{0,1:T(8,128)S(1)} fusion(f32[512,512]{0,1:T(8,128)S(1)} %copy.9, f32[768,512]{1,0:T(8,128)} %pg.1, bf16[768,512]{1,0:T(8,128)(2,1)} %panel.1, f32[512,512]{1,0:T(8,128)S(1)} %copy-done.7), kind=kOutput, calls=%fused_computation.1 | convolution fusion | flops 2416443392 | bytes 5505024 | tf_op jit(solution)/shard_map/dot_general | solution.py:18
  237.7 0.3 copy.10
  238.0 1.3 reshape.14.x
  239.3 46.6 %shard_map.70 = f32[4,8,8,1024]{3,2,1,0:T(8,128)} custom-call(f32[4,8,8,1024]{3,2,1,0:T(8,128)} %reshape.14.x), custom_call_target="tpu_custom_call" | custom-call | tf_op jit(solution)/shard_map/pallas_call | solution.py:476
  286.0 0.0 copy-start.1
  286.0 0.0 copy-start.4
  286.0 1.6 reshape.15.s_ref
  287.6 0.0 copy-done.6
  287.6 0.0 copy-done.1
  287.6 0.3 copy-done.4
  287.8 12.5 %shard_map.71 = f32[512,512]{1,0:T(8,128)} custom-call(f32[512,512]{1,0:T(8,128)S(1)} %reshape.15.s_ref, f32[512,512]{1,0:T(8,128)S(1)} %copy-done.4, f32[512,512]{1,0:T(8,128)S(1)} %copy-done.1, f32[4,128,128]{2,1,0:T(8,128)S(1)} %copy-done.6), custom_call_target="tpu_custom_call" | custom-call | tf_op jit(solution)/shard_map/pallas_call | solution.py:535
  (5 shorter events, 0.0 us)
Async XLA Ops:
  0.6 2.4 copy-start.8
  222.2 1.2 copy-start
  223.5 1.4 copy-start.2
  224.9 1.4 copy-start.3
  226.3 0.9 copy-start.5
  227.2 7.0 %copy-start.7 = (f32[512,512]{1,0:T(8,128)S(1)}, f32[512,512]{1,0:T(8,128)}, u32[]{:S(2)}) copy-start(f32[512,512]{1,0:T(8,128)} %get-tuple-element.9) | copy-start | bytes 3145732
  239.3 48.2 %copy-start.6 = (f32[4,128,128]{2,1,0:T(8,128)S(1)}, f32[4,128,128]{2,1,0:T(8,128)}, u32[]{:S(2)}) copy-start(f32[4,128,128]{2,1,0:T(8,128)} %get-tuple-element.8.inv) | copy-start | bytes 786436
  286.0 1.6 copy-start.1
  286.0 1.8 copy-start.4

commit v2 on v1

--- a/solution.py
+++ b/solution.py
@@ -10,6 +10,7 @@
 F32, BF16 = jnp.float32, jnp.bfloat16
 VMEM_LIMIT = 66_000_000
 NB = 4
+EARLY = 2
 BLK = 128
 HI = lax.Precision.HIGHEST
 
@@ -18,6 +19,10 @@
     return lax.dot_general(
         a, b, (((ca,), (cb,)), ((), ())), precision=precision, preferred_element_type=F32
     )
+
+
+def lower_blocks(count):
+    return [(i, j) for i in range(count) for j in range(i + 1)]
 
 
 def invert_blocks(l_ref, inv_ref):
@@ -43,9 +48,9 @@
 
 def main_kernel(
     n_row, n_col, G, panel, panel_t, pg, low,
-    dt_out, t_out, q_out, inv_out, pr, rl, tr,
-    colp, rowp, gbuf, tacc, dsum, dpart, stage,
-    gsem, cs, cr, zs, zr, ps, prr, ds, dr, rs, rr, ts, trs, lsem,
+    dg, adj_out, diag_out, pr, rl, tr,
+    colp, rowp, gbuf, tacc, dsum, dpart, stage, q_out, inv_out, own_t, sx, s_in, s_row, s_col, s_all,
+    gsem, cs, cr, zs, zr, ps, prr, ds, dr, rs, rr, ts, trs, s1, r1, s2, r2, s3, r3, s4, r4, lsem,
 ):
     nz = n_col // 2
     r, c = lax.axis_index("row"), lax.axis_index("col")
@@ -57,19 +62,22 @@
     def dev(row, col):
         return dict(device_id=(row, col), device_id_type=pl.DeviceIdType.MESH)
 
+    rest = n_col - 2
+    end_a = 2 * n_row
+    end_d = end_a + 2 * EARLY * n_row
+    end_t = end_d + rest * n_row
+
     def tile_of(s):
-        t = s - 2 * n_row
+        t = jnp.maximum(jnp.where(s < end_t, s - end_a, s - end_t + 2 * EARLY * n_row), 0)
         i = t // n_row
-        z_d = z_order(i // 2)
-        c_d = 2 * z_d + jnp.where(i % 2 == 0, 1 - k, k)
-        u = t - n_row * n_col
-        rest = n_col - 2
-        v = jnp.maximum(u, 0)
+        c_d = 2 * z_order(i // 2) + jnp.where(i % 2 == 0, 1 - k, k)
+        v = jnp.maximum(s - end_d, 0)
         a_b = (r + 1 + v // rest) % n_row
         jj = v % rest
         c_b = 2 * ((z + 1 + jj // 2) % nz) + jj % 2
-        a = jnp.where(u >= 0, a_b, jnp.where(t >= 0, jnp.maximum(t, 0) % n_row, s % n_row))
-        col = jnp.where(u >= 0, c_b, jnp.where(t >= 0, c_d, jnp.where(s < n_row, c, other)))
+        in_t = (s >= end_d) & (s < end_t)
+        a = jnp.where(in_t, a_b, jnp.where(s < end_a, s % n_row, t % n_row))
+        col = jnp.where(in_t, c_b, jnp.where(s >= end_a, c_d, jnp.where(s < n_row, c, other)))
         return a, col
 
     def z_order(i):
@@ -102,18 +110,9 @@
     barrier = pltpu.get_barrier_semaphore()
     for d in range(1, n_row):
         pl.semaphore_signal(barrier, inc=1, **dev((r + d) % n_row, c))
-    pl.semaphore_signal(barrier, inc=1, **dev(r, other))
-
-    @pl.when(z > 0)
-    def _():
-        pl.semaphore_signal(barrier, inc=1, **dev(r, c - 2))
-
-    @pl.when(z < last)
-    def _():
-        pl.semaphore_signal(barrier, inc=1, **dev(r, c + 2))
-
-    near = jnp.where(z > 0, 1, 0) + jnp.where(z < last, 1, 0)
-    pl.semaphore_wait(barrier, n_row + near)
+    for d in range(1, n_col):
+        pl.semaphore_signal(barrier, inc=1, **dev(r, (c + d) % n_col))
+    pl.semaphore_wait(barrier, n_row + n_col - 2)
 
     def col_send(d):
         return pltpu.make_async_remote_copy(
@@ -191,6 +190,12 @@
     pair_wait(z)
     lax.fori_loop(n_row, 2 * n_row, t_step, 0)
     invert_blocks(low, inv_out)
+    own_t[...] = jnp.zeros(own_t.shape, F32)
+    left_over = pg[...]
+    for _ in range(3):
+        piece = left_over.astype(BF16)
+        own_t[...] += dot(panel_t[...], piece)
+        left_over = left_over - piece.astype(F32)
     relay(1)
     for d in range(1, n_row):
         pltpu.make_async_remote_copy(
@@ -244,19 +249,21 @@
 
         lax.fori_loop(0, n_row, step, 0)
 
-    base = 2 * n_row
-    for i in range(nz):
+    def d_pair(i, base):
         zb = z_order(i)
         slot = i % 2
         if i >= 2:
             part_send(z_order(i - 2), slot).wait_send()
-        d_into(base + 2 * i * n_row, dpart.at[slot])
+        d_into(base, dpart.at[slot])
         part_send(zb, slot).start()
-        d_into(base + (2 * i + 1) * n_row, dsum.at[zb])
+        d_into(base + n_row, dsum.at[zb])
         presum(i)
+
+    for i in range(EARLY):
+        d_pair(i, end_a + 2 * i * n_row)
         if i + 2 < nz:
             relay(i + 2)
-    for h in range(nz + 1, nz):
+    for h in range(EARLY + 2, nz):
         relay(h)
 
     def wait_others(d, carry):
@@ -271,12 +278,10 @@
             tacc.at[a], tr.at[r], ts.at[d], trs.at[d], **dev(a, c)
         )
 
-    base = 2 * n_row + n_row * n_col
-    rest = n_col - 2
     for i in range(n_row):
-        lax.fori_loop(base + i * rest, base + (i + 1) * rest, t_step, 0)
-        if i < n_row - 1:
-            t_send(i + 1).start()
+        lax.fori_loop(end_d + i * rest, end_d + (i + 1) * rest, t_step, 0)
+        if i == 0:
+            t_send(1).start()
 
     q_out[...] = jnp.zeros(q_out.shape, F32)
 
@@ -289,6 +294,52 @@
 
     lax.fori_loop(0, n_row, q_step, 0)
 
+    for n, (i, j) in enumerate(lower_blocks(q_out.shape[0] // BLK)):
+        bi, bj = slice(i * BLK, (i + 1) * BLK), slice(j * BLK, (j + 1) * BLK)
+        sx[n * BLK : (n + 1) * BLK, :] = (own_t[bj, bi] - q_out[bj, bi]).T - q_out[bi, bj]
+
+    remote = pltpu.make_async_remote_copy
+    length = s_row.shape[0]
+    short = s_col.shape[0]
+
+    def longs(ref, row):
+        return ref.at[pl.ds(pl.multiple_of(row * length, 8), length)]
+
+    def shorts(ref, col, row=None):
+        start = col * short if row is None else row * length + col * short
+        return ref.at[pl.ds(pl.multiple_of(start, 8), short)]
+
+    row_at = lambda d: (r + d) % n_row
+    col_at = lambda d: (c + d) % n_col
+    one = [
+        remote(longs(sx, row_at(d)), s_in.at[d], s1.at[d], r1.at[d], **dev(row_at(d), c))
+        for d in range(1, n_row)
+    ]
+    two = [
+        remote(shorts(s_row, col_at(d)), s_in.at[0, pl.ds(d * short, short)], s2.at[d], r2.at[d],
+               **dev(r, col_at(d)))
+        for d in range(1, n_col)
+    ]
+    three = [
+        remote(shorts(s_all, c, r), shorts(s_all, c, r), s3.at[d], r3.at[d], **dev(r, col_at(d)))
+        for d in range(1, n_col)
+    ]
+    four = [
+        remote(longs(s_all, r), longs(s_all, r), s4.at[d], r4.at[d], **dev(row_at(d), c))
+        for d in range(1, n_row)
+    ]
+
+    def start_all(copies):
+        for cp in copies:
+            cp.start()
+
+    start_all(one)
+    for d in range(2, n_row):
+        t_send(d).start()
+
+    for i in range(EARLY, nz):
+        d_pair(i, end_t + 2 * (i - EARLY) * n_row)
+
     def hop(way, zb):
         sum_wait = pltpu.make_async_remote_copy(
             stage, rl.at[way, zb], rs.at[way, zb], rr.at[way, zb], **dev(r, other)
@@ -296,25 +347,42 @@
         sum_wait.wait_recv()
         add_in(dsum.at[zb], rl.at[way, zb])
 
+    def pass_up(zb):
+        @pl.when((z > 0) & (zb > z))
+        def _():
+            hop(0, zb)
+            sum_send(0, zb).start()
+
+    def pass_down(zb, side):
+        @pl.when((z < last) & (zb < z) & side)
+        def _():
+            hop(1, zb)
+            sum_send(1, zb).start()
+
     for q in range(nz):
-        up = last - q
-
-        @pl.when((z > 0) & (up > z))
-        def _():
-            hop(0, up)
-            sum_send(0, up).start()
-
-        @pl.when((z < last) & (q < z))
-        def _():
-            hop(1, q)
-            sum_send(1, q).start()
+        if q == 1:
+            s_row[...] = longs(sx, r)[...]
+            for d in range(1, n_row):
+                one[d - 1].wait_recv()
+                s_row[...] += s_in[d]
+            start_all(two)
+        pass_down(q, z >= nz // 2)
+        pass_up(last - q)
+        pass_down(q, z < nz // 2)
+
+    s_col[...] = shorts(s_row, c)[...]
+    for d in range(1, n_col):
+        two[d - 1].wait_recv()
+        s_col[...] += s_in[0, d * short : (d + 1) * short, :]
+    shorts(s_all, c, r)[...] = s_col[...]
+    start_all(three)
 
     def fetch(src, dst):
         cp = pltpu.make_async_copy(src, dst, lsem)
         cp.start()
         cp.wait()
 
-    t_out[...] = pg[...] - tacc[r]
+    tacc[r] = pg[...] - tacc[r]
     tbuf = tacc.at[(r + 1) % n_row]
     for d in range(1, n_row):
         t_send(d).wait_send()
@@ -324,7 +392,14 @@
             tacc.at[src], tr.at[src], ts.at[d], trs.at[d], **dev((r + d) % n_row, c)
         ).wait_recv()
         fetch(tr.at[src], tbuf)
-        t_out[...] -= tbuf[...]
+        tacc[r] -= tbuf[...]
+
+    for d in range(1, n_col):
+        remote(
+            shorts(s_all, c, r), shorts(s_all, col_at(n_col - d), r), s3.at[d], r3.at[d],
+            **dev(r, col_at(d)),
+        ).wait_recv()
+    start_all(four)
 
     @pl.when(z > 0)
     def _():
@@ -334,7 +409,19 @@
     def _():
         hop(1, z)
 
-    dt_out[...] = dsum[z]
+    adj_out[...] = right_blocks(tacc[r] - dsum[z].T, low, inv_out)
+    for d in range(1, n_row):
+        remote(
+            longs(s_all, r), longs(s_all, row_at(n_row - d)), s4.at[d], r4.at[d],
+            **dev(row_at(d), c),
+        ).wait_recv()
+    blocks = q_out.shape[0] // BLK
+    q_out[...] = jnp.zeros(q_out.shape, F32)
+    for n, (i, j) in enumerate(lower_blocks(blocks)):
+        q_out[i * BLK : (i + 1) * BLK, j * BLK : (j + 1) * BLK] = s_all[n * BLK : (n + 1) * BLK, :]
+    diag_kernel(q_out, dg, low, inv_out, diag_out)
+    for cp in one + two + three + four:
+        cp.wait_send()
 
     for d in range(1, n_row):
         col_send(d).wait_send()
@@ -364,24 +451,26 @@
         part_send(z_order(i), i % 2).wait_send()
 
 
-def main_call(G, panel, pg, low, n_row, n_col):
+def main_call(G, panel, pg, low, dg, n_row, n_col):
     g, b = panel.shape
     nz = n_col // 2
+    entries = len(lower_blocks(b // BLK)) * BLK
     vm = pl.BlockSpec(memory_space=pltpu.VMEM)
     hbm = pl.BlockSpec(memory_space=pl.ANY)
     dma = pltpu.SemaphoreType.DMA
     sds = jax.ShapeDtypeStruct
     sizes = [(NB,), (n_row,), (n_row,), (2, nz + 1), (2, nz + 1), (nz,), (nz,), (2,), (nz,),
-             (2, nz), (2, nz), (n_row,), (n_row,)]
+             (2, nz), (2, nz), (n_row,), (n_row,), (n_row,), (n_row,), (n_col,), (n_col,), (n_col,), (n_col,),
+             (n_row,), (n_row,)]
     flops = 4 * G.shape[0] * G.shape[1] * b
     outs = pl.pallas_call(
         functools.partial(main_kernel, n_row, n_col),
         out_shape=[
-            sds((b, g), F32), sds((g, b), F32), sds((b, b), F32), sds((b // BLK, BLK, BLK), F32),
+            sds((g, b), F32), sds((b, b), F32),
             sds((nz, b, g), F32), sds((2, nz, b, g), F32), sds((n_row, g, b), F32),
         ],
-        in_specs=[hbm, vm, vm, vm, vm],
-        out_specs=[vm, vm, vm, vm, hbm, hbm, hbm],
+        in_specs=[hbm, vm, vm, vm, vm, vm],
+        out_specs=[vm, vm, hbm, hbm, hbm],
         scratch_shapes=[
             pltpu.VMEM((n_row, b, g), BF16),
             pltpu.VMEM((n_col, g, b), BF16),
@@ -390,6 +479,14 @@
             pltpu.VMEM((nz, b, g), F32),
             pltpu.VMEM((2, b, g), F32),
             pltpu.VMEM((b, g), F32),
+            pltpu.VMEM((b, b), F32),
+            pltpu.VMEM((b // BLK, BLK, BLK), F32),
+            pltpu.VMEM((b, b), F32),
+            pltpu.VMEM((entries, BLK), F32),
+            pltpu.VMEM((n_row, entries // n_row, BLK), F32),
+            pltpu.VMEM((entries // n_row, BLK), F32),
+            pltpu.VMEM((entries // n_row // n_col, BLK), F32),
+            pltpu.VMEM((entries, BLK), F32),
         ]
         + [dma(s) for s in sizes]
         + [dma],
@@ -397,96 +494,8 @@
             collective_id=0, has_side_effects=True, vmem_limit_bytes=VMEM_LIMIT
         ),
         cost_estimate=pl.CostEstimate(flops=flops, bytes_accessed=4 * G.size, transcendentals=0),
-    )(G, panel, panel.T, pg, low)
-    return outs[:4]
-
-
-def sum_kernel(n_row, n_col, x, out, a_in, a_sum, b_in, s1, r1, s2, r2, s3, r3, s4, r4):
-    r, c = lax.axis_index("row"), lax.axis_index("col")
-
-    def dev(row, col):
-        return dict(device_id=(row, col), device_id_type=pl.DeviceIdType.MESH)
-
-    def row_at(d):
-        return lax.rem(r + d, n_row)
-
-    def col_at(d):
-        return lax.rem(c + d, n_col)
-
-    barrier = pltpu.get_barrier_semaphore()
-    for d in range(1, n_row):
-        pl.semaphore_signal(barrier, inc=1, **dev(row_at(d), c))
-    for d in range(1, n_col):
-        pl.semaphore_signal(barrier, inc=1, **dev(r, col_at(d)))
-    pl.semaphore_wait(barrier, n_row + n_col - 2)
-
-    remote = pltpu.make_async_remote_copy
-    one = [
-        remote(x.at[row_at(d)], a_in.at[d], s1.at[d], r1.at[d], **dev(row_at(d), c))
-        for d in range(1, n_row)
-    ]
-    for cp in one:
-        cp.start()
-    a_sum[...] = x[r]
-    for cp, d in zip(one, range(1, n_row)):
-        cp.wait_recv()
-        a_sum[...] += a_in[d]
-    two = [
-        remote(a_sum.at[col_at(d)], b_in.at[d], s2.at[d], r2.at[d], **dev(r, col_at(d)))
-        for d in range(1, n_col)
-    ]
-    for cp in two:
-        cp.start()
-    acc = a_sum[c]
-    for cp, d in zip(two, range(1, n_col)):
-        cp.wait_recv()
-        acc += b_in[d]
-    out[r, c] = acc
-    three = [
-        remote(out.at[r, c], out.at[r, c], s3.at[d], r3.at[d], **dev(r, col_at(d)))
-        for d in range(1, n_col)
-    ]
-    for cp in three:
-        cp.start()
-    for d in range(1, n_col):
-        remote(
-            out.at[r, c], out.at[r, col_at(n_col - d)], s3.at[d], r3.at[d], **dev(r, col_at(d))
-        ).wait_recv()
-    four = [
-        remote(out.at[r], out.at[r], s4.at[d], r4.at[d], **dev(row_at(d), c))
-        for d in range(1, n_row)
-    ]
-    for cp in four:
-        cp.start()
-    for d in range(1, n_row):
-        remote(
-            out.at[r], out.at[row_at(n_row - d)], s4.at[d], r4.at[d], **dev(row_at(d), c)
-        ).wait_recv()
-    for cp in one + two + three + four:
-        cp.wait_send()
-
-
-def sum_call(x, n_row, n_col):
-    shape = x.shape
-    w = x.size // (n_row * n_col * 8)
-    x = x.reshape(n_row, n_col, 8, w)
-    vm = pl.BlockSpec(memory_space=pltpu.VMEM)
-    dma = pltpu.SemaphoreType.DMA
-    row, col = dma((n_row,)), dma((n_col,))
-    out = pl.pallas_call(
-        functools.partial(sum_kernel, n_row, n_col),
-        out_shape=jax.ShapeDtypeStruct(x.shape, F32),
-        in_specs=[vm],
-        out_specs=vm,
-        scratch_shapes=[
-            pltpu.VMEM((n_row, n_col, 8, w), F32),
-            pltpu.VMEM((n_col, 8, w), F32),
-            pltpu.VMEM((n_col, 8, w), F32),
-            row, row, col, col, col, col, row, row,
-        ],
-        compiler_params=pltpu.CompilerParams(collective_id=1, has_side_effects=True),
-    )(x)
-    return out.reshape(shape)
+    )(G, panel, panel.T, pg, low, dg)
+    return tuple(outs[:2])
 
 
 def right_blocks(rhs, low, inv):
@@ -520,9 +529,9 @@
 
 
 def diag_kernel(s_ref, dg, low, inv, out):
-    lower, inverse = low[...], inv[...]
-    rows = lax.broadcasted_iota(jnp.int32, lower.shape, 0)
-    cols = lax.broadcasted_iota(jnp.int32, lower.shape, 1)
+    rows = lax.broadcasted_iota(jnp.int32, low.shape, 0)
+    cols = lax.broadcasted_iota(jnp.int32, low.shape, 1)
+    lower, inverse = jnp.where(rows >= cols, low[...], 0.0), inv[...]
     diag_new = dg[...] - left_blocks(s_ref[...], lower, inverse)
     inner = dot(lower, jnp.where(rows >= cols, diag_new, 0.0), 0, 0, precision=HI)
     inner = inner * jnp.where(rows > cols, 1.0, jnp.where(rows == cols, 0.5, 0.0))
@@ -555,13 +564,14 @@
 
 def on_device(n_row, n_col, trailing_grad, panel, panel_grad, diag_factor, diag_grad):
     local_flip = trailing_grad.reshape(-1, trailing_grad.shape[3])
+    g, b = panel.shape
+    shares = len(lower_blocks(b // BLK)) * BLK % (8 * n_row * n_col)
+    if g % 128 == 0 and shares == 0 and n_col % 2 == 0 and n_col >= 4:
+        return main_call(local_flip, panel, panel_grad, diag_factor, diag_grad, n_row, n_col)
     lower = jnp.tril(diag_factor)
+    dt, t, q, inv = plain_products(local_flip, panel, panel_grad, lower)
     own = dot(panel_grad, panel.astype(F32), 0, 0, precision=HI)
-    if panel.shape[0] % 128 == 0 and n_col % 2 == 0 and n_col > 2:
-        dt, t, q, inv = main_call(local_flip, panel, panel_grad, lower, n_row, n_col)
-    else:
-        dt, t, q, inv = plain_products(local_flip, panel, panel_grad, lower)
-    total = sum_call(own - q - q.T, n_row, n_col)
+    total = lax.psum(own - q - q.T, ("row", "col"))
     panel_adj = local_call(panel_kernel, panel_grad.shape, t, dt, lower, inv)
     diag_adj = local_call(diag_kernel, lower.shape, total, diag_grad, lower, inv)
     return (panel_adj, diag_adj)

time: 301 us -> 218 us (0.72)
  Pallas kernels: 284 us -> 210 us
  local copies, waits for them, and re-layouts: 11.2 us -> 7.22 us
  matrix products: 3.11 us -> 0 us
    pallas_call x3 -> x0, Pallas kernels: 66.1 us -> none  [the longest x1 46.6 us: sum_call(): pl.pallas_call(functools.partial(sum_kernel, n_row, n_col), out_shape=jax...]
    pallas_call x1, Pallas kernels: 218 us -> 210 us  [main_call(): pl.pallas_call(functools.partial(main_kernel, n_row, n_col), out_shape=[s...]
    dot_general x1 -> x0, matrix products: 3.11 us -> none  [dot(): lax.dot_general(a, b, (((ca,), (cb,)), ((), ())), precision=precision, pr...]
    unnamed x19 -> x3, local copies, waits for them, and re-layouts: 7.64 us -> 7.22 us
where the time goes in v2:
time: 218 us
  Pallas kernels  210 us (96%)
  local copies, waits for them, and re-layouts  7.22 us (3%)
    pallas_call x1, Pallas kernels, main_call(): pl.pallas_call(functools.partial(main_kernel, n_row, n_col), out_shape=[s...  210 us
    unnamed x3, local copies, waits for them, and re-layouts  7.22 us

profile of v2, /device:TPU:0, one launch (start us, length us, event | category | flops | bytes accessed | tf_op | source)
XLA Modules:
  0.0 217.7 jit_solution(2880989565358758226)
XLA Ops:
  0.6 2.3 %copy.7 = bf16[768,512]{0,1:T(8,128)(2,1)} copy(bf16[768,512]{1,0:T(8,128)(2,1)} %panel.1) | data formatting | bytes 1572864 | tf_op args[1]
  2.9 209.9 %shard_map.68 = (f32[768,512]{1,0:T(8,128)}, f32[512,512]{1,0:T(8,128)}, f32[4,512,768]{2,1,0:T(8,128)}, f32[2,4,512,768]{3,2,1,0:T(8,128)}, f32[4,768,512]{2,1,0:T(8,128)}) custom-call(bf16[3072,6144]{1,0:T(8,128)(2,1)} %bitcast.3, bf16[768,512]{1,0:T(8,128)(2,1)} %panel.1, bf16[512,768]{1,0:T(8,128)(2,1)} %bitcast.2, f32[768,512]{1,0:T(8,128)} %pg.1, ...), custom_call_target="tpu_custom_call" | custom-call | flops 38654705664 | bytes 75497472 | tf_op jit(solution)/shard_map/pallas_call | solution.py:466
  212.8 2.7 %copy.10 = f32[768,512]{1,0:T(8,128)} copy(f32[768,512]{1,0:T(8,128)} %get-tuple-element.8) | data formatting | bytes 3145728
  215.5 2.3 %copy.11 = f32[512,512]{1,0:T(8,128)} copy(f32[512,512]{1,0:T(8,128)} %get-tuple-element.9) | data formatting | bytes 2097152

commit v3 on v2

--- a/solution.py
+++ b/solution.py
@@ -249,7 +249,7 @@
 
         lax.fori_loop(0, n_row, step, 0)
 
-    def d_pair(i, base):
+    def d_pair(i, base, between=None):
         zb = z_order(i)
         slot = i % 2
         if i >= 2:
@@ -257,6 +257,8 @@
         d_into(base, dpart.at[slot])
         part_send(zb, slot).start()
         d_into(base + n_row, dsum.at[zb])
+        if between is not None:
+            between()
         presum(i)
 
     for i in range(EARLY):
@@ -337,8 +339,17 @@
     for d in range(2, n_row):
         t_send(d).start()
 
+    def along_col():
+        s_row[...] = longs(sx, r)[...]
+        for d in range(1, n_row):
+            one[d - 1].wait_recv()
+            s_row[...] += s_in[d]
+        start_all(two)
+
     for i in range(EARLY, nz):
-        d_pair(i, end_t + 2 * (i - EARLY) * n_row)
+        d_pair(i, end_t + 2 * (i - EARLY) * n_row, along_col if i == EARLY else None)
+    if nz <= EARLY:
+        along_col()
 
     def hop(way, zb):
         sum_wait = pltpu.make_async_remote_copy(
@@ -360,12 +371,6 @@
             sum_send(1, zb).start()
 
     for q in range(nz):
-        if q == 1:
-            s_row[...] = longs(sx, r)[...]
-            for d in range(1, n_row):
-                one[d - 1].wait_recv()
-                s_row[...] += s_in[d]
-            start_all(two)
         pass_down(q, z >= nz // 2)
         pass_up(last - q)
         pass_down(q, z < nz // 2)
@@ -377,6 +382,13 @@
     shorts(s_all, c, r)[...] = s_col[...]
     start_all(three)
 
+    for d in range(1, n_col):
+        remote(
+            shorts(s_all, c, r), shorts(s_all, col_at(n_col - d), r), s3.at[d], r3.at[d],
+            **dev(r, col_at(d)),
+        ).wait_recv()
+    start_all(four)
+
     def fetch(src, dst):
         cp = pltpu.make_async_copy(src, dst, lsem)
         cp.start()
@@ -393,13 +405,6 @@
         ).wait_recv()
         fetch(tr.at[src], tbuf)
         tacc[r] -= tbuf[...]
-
-    for d in range(1, n_col):
-        remote(
-            shorts(s_all, c, r), shorts(s_all, col_at(n_col - d), r), s3.at[d], r3.at[d],
-            **dev(r, col_at(d)),
-        ).wait_recv()
-    start_all(four)
 
     @pl.when(z > 0)
     def _():

time: 218 us -> 235 us (1.078)
  Pallas kernels: 210 us -> 227 us
    pallas_call x1, Pallas kernels: 210 us -> 227 us  [main_call(): pl.pallas_call(functools.partial(main_kernel, n_row, n_col), out_shape=[s...]
where the time goes in v3:
time: 235 us
  Pallas kernels  227 us (97%)
  local copies, waits for them, and re-layouts  7.22 us (3%)
    pallas_call x1, Pallas kernels, main_call(): pl.pallas_call(functools.partial(main_kernel, n_row, n_col), out_shape=[s...  227 us
    unnamed x3, local copies, waits for them, and re-layouts  7.22 us

profile of v3, /device:TPU:0, one launch (start us, length us, event | category | flops | bytes accessed | tf_op | source)
XLA Modules:
  0.0 234.6 jit_solution(17035037241464443198)
XLA Ops:
  0.6 2.3 copy.7
  2.9 226.8 %shard_map.68 = (f32[768,512]{1,0:T(8,128)}, f32[512,512]{1,0:T(8,128)}, f32[4,512,768]{2,1,0:T(8,128)}, f32[2,4,512,768]{3,2,1,0:T(8,128)}, f32[4,768,512]{2,1,0:T(8,128)}) custom-call(bf16[3072,6144]{1,0:T(8,128)(2,1)} %bitcast.3, bf16[768,512]{1,0:T(8,128)(2,1)} %panel.1, bf16[512,768]{1,0:T(8,128)(2,1)} %bitcast.2, f32[768,512]{1,0:T(8,128)} %pg.1, ...), custom_call_target="tpu_custom_call" | custom-call | flops 38654705664 | bytes 75497472 | tf_op jit(solution)/shard_map/pallas_call | solution.py:471
  229.7 2.7 %copy.10 = f32[768,512]{1,0:T(8,128)} copy(f32[768,512]{1,0:T(8,128)} %get-tuple-element.8) | data formatting | bytes 3145728
  232.4 2.3 copy.11
